TPU v7x, 256 devices: a whole 4x4x8 slice. The times are simulated.
256 devices in a mesh: dp: 128 (over y, z, x), tensor: 2 (over core).
Axes of the slice: x: 4, y: 4, z: 8, core: 2. Of those that a mesh axis runs over, the one named last changes fastest.
Arguments:
- fc_grads: bfloat16 [128, 768, 3072], P('dp', None, 'tensor')
- fc_error: bfloat16 [128, 768, 3072], P('dp', None, 'tensor'), may hold values from -4 to 4
- query: float32 [3072, 32], P('tensor'), may hold values from -0.109375 to 0.109375
- gram_inverse: float32 [32, 32], replicated
- fc_master: float32 [768, 3072], P('dp', 'tensor'), may hold values from -6 to 6
- fc_momentum: float32 [768, 3072], P('dp', 'tensor'), may hold values from -3 to 3
- vec_grads: bfloat16 [128, 5376], P('dp'), may hold values from -24 to 24
- vec_master: float32 [5376], P('dp'), may hold values from -6 to 6
- vec_momentum: float32 [5376], P('dp'), may hold values from -4 to 4
Outputs:
- new_error: bfloat16 [128, 768, 3072], P('dp', None, 'tensor')
- new_momentum: float32 [768, 3072], P('dp', 'tensor')
- new_master: float32 [768, 3072], P('dp', 'tensor')
- new_weights: bfloat16 [768, 3072], P(None, 'tensor')
- vec_new_momentum: float32 [5376], P('dp')
- vec_new_master: float32 [5376], P('dp')
- vec_weights: bfloat16 [5376], replicated
All inputs are finite; a program needn't handle non-finite values.
Results may differ from a plain program's by a relative error of at most 0.0085.
Values may be sent and summed in bfloat16 or wider, within the bound.
No kernel may reach another device: no remote copies, remote signals or barrier semaphores. Data moves between devices by JAX's collectives and lax.ppermute only.
A program may use at most 64 MiB of HBM per device.

v0:
```python
import jax
import jax.numpy as jnp
from jax import lax
from jax.sharding import PartitionSpec as P

momentum_decay = 0.9
step_size = 0.5


def on_device(
    fc_grads,
    fc_error,
    query,
    gram_inverse,
    fc_master,
    fc_momentum,
    vec_grads,
    vec_master,
    vec_momentum,
):
    replicas = lax.axis_size("dp")
    replica_index = lax.axis_index("dp")
    merged = (fc_grads[0].astype(jnp.float32) + fc_error[0].astype(jnp.float32)).astype(
        jnp.bfloat16
    )
    query_b = query.astype(jnp.bfloat16)
    row_part = jnp.dot(merged, query_b, preferred_element_type=jnp.float32)
    vec_term = vec_grads[0].astype(jnp.float32)
    shard_len = vec_master.shape[0]
    row_total = lax.psum(row_part, ("dp", "tensor"))
    vec_total = lax.psum(vec_term, "dp")
    vec_mean = (
        lax.dynamic_slice_in_dim(vec_total, replica_index * shard_len, shard_len, 0) / replicas
    )
    row_mean = row_total / replicas
    row_basis = jnp.dot(row_mean, gram_inverse, precision=lax.Precision.HIGHEST)
    basis_b = row_basis.astype(jnp.bfloat16)
    col_part = lax.dot_general(
        merged, basis_b, (((0,), (0,)), ((), ())), preferred_element_type=jnp.float32
    )
    col_mean = lax.psum(col_part, "dp") / replicas
    approx = jnp.dot(row_basis, col_mean.T, precision=lax.Precision.HIGHEST)
    new_error = (merged.astype(jnp.float32) - approx).astype(jnp.bfloat16)[None]
    state_rows = fc_master.shape[0]
    basis_rows = lax.dynamic_slice_in_dim(row_basis, replica_index * state_rows, state_rows, 0)
    approx_rows = jnp.dot(basis_rows, col_mean.T, precision=lax.Precision.HIGHEST)
    new_momentum = momentum_decay * fc_momentum + approx_rows
    new_master = fc_master - step_size * (approx_rows + momentum_decay * new_momentum)
    vec_new_momentum = momentum_decay * vec_momentum + vec_mean
    vec_new_master = vec_master - step_size * (vec_mean + momentum_decay * vec_new_momentum)
    new_weights, vec_weights = (
        lax.all_gather(new_master.astype(jnp.bfloat16), "dp", axis=0, tiled=True),
        lax.all_gather(vec_new_master.astype(jnp.bfloat16), "dp", axis=0, tiled=True),
    )
    return (
        new_error,
        new_momentum,
        new_master,
        new_weights,
        vec_new_momentum,
        vec_new_master,
        vec_weights,
    )


def solution(mesh):
    return jax.shard_map(
        on_device,
        mesh=mesh,
        in_specs=(
            P("dp", None, "tensor"),
            P("dp", None, "tensor"),
            P("tensor", None),
            P(),
            P("dp", "tensor"),
            P("dp", "tensor"),
            P("dp", None),
            P("dp"),
            P("dp"),
        ),
        out_specs=(
            P("dp", None, "tensor"),
            P("dp", "tensor"),
            P("dp", "tensor"),
            P(None, "tensor"),
            P("dp"),
            P("dp"),
            P(),
        ),
        check_vma=False,
    )
```

profile of v0, /device:TPU:0, one launch (start us, length us, event | category | flops | bytes accessed | tf_op | source)
XLA Modules:
  0.0 1860.5 jit_solution(18031364214805871848)
XLA Ops:
  7.2 0.0 copy-start
  7.2 0.0 copy-start.1
  7.2 0.0 all-reduce.4.cloned.1.call-start
  7.2 4.0 fusion.9
  11.2 0.0 all-reduce.4.cloned.1.call-update
  11.2 0.0 all-reduce.6.cloned.1.call-start
  11.3 244.5 %all-reduce.4.cloned.1.call-done = f32[768,32]{0,1:T(8,128)} async-done(((f32[768,32]{0,1:T(8,128)}), f32[768,32]{0,1:T(8,128)}) %all-reduce.4.cloned.1.call-update) | async-done | bytes 98320 | tf_op jit(solution)/shard_map/psum | solution.py:30
  255.8 0.0 copy-done
  255.8 1.2 fusion.7
  256.9 0.0 copy-done.1
  256.9 0.0 copy-start.2
  257.0 0.0 copy-start.3
  257.0 0.0 copy-start.7
  257.0 0.0 copy-start.4
  257.0 0.0 copy-start.5
  257.0 0.0 copy-start.6
  257.0 3.1 fusion.11
  260.1 0.0 all-reduce.6.cloned.1.call-update
  260.1 0.0 all-gather.3.cloned.1.call-start
  260.2 209.9 %all-reduce.6.cloned.1.call-done = f32[1536,32]{0,1:T(8,128)} async-done(((f32[1536,32]{0,1:T(8,128)}), f32[1536,32]{0,1:T(8,128)}) %all-reduce.6.cloned.1.call-update) | async-done | bytes 196624 | tf_op jit(solution)/shard_map/psum | solution.py:41
  470.1 1.9 convert_bitcast_fusion
  472.0 0.0 all-gather.3.cloned.1.call-update
  472.0 0.0 copy-done.7
  472.0 0.6 dynamic-slice
  473.3 0.1 convert_reduce_fusion
  473.4 686.4 %psum.23 = f32[5376]{0:T(1024)S(1)} all-reduce(f32[5376]{0:T(1024)S(1)} %convert_reduce_fusion), channel_id=1, replica_groups=mesh['dp'=128,'tensor'=2] {'dp'}, use_global_device_ids=true, to_apply=%region_2.0 | all-reduce | flops 5376 | bytes 43008 | tf_op jit(solution)/shard_map/psum | solution.py:31
  1159.7 0.0 copy-done.5
  1159.7 0.6 fusion.21
  1160.3 0.2 dynamic-update-slice
  1160.5 681.7 %all-reduce = bf16[5376]{0:T(1024)(128)(2,1)} all-reduce(bf16[5376]{0:T(1024)(128)(2,1)S(1)} %dynamic-update-slice), channel_id=1, replica_groups=mesh['dp'=128,'tensor'=2] {'dp'}, use_global_device_ids=true, to_apply=%add | all-reduce | flops 5376 | bytes 21504
  1842.3 6.6 fusion
  1848.9 5.0 reshape.25
  (6 shorter events, 0.0 us)
Async XLA Ops:
  7.2 248.6 %copy-start = (f32[32,32]{1,0:T(8,128)S(1)}, f32[32,32]{1,0:T(8,128)}, u32[]{:S(2)}) copy-start(f32[32,32]{1,0:T(8,128)} %param.12) | copy-start | bytes 12292
  7.2 249.8 %copy-start.1 = (bf16[1,768,1536]{2,1,0:T(8,128)(2,1)S(1)}, bf16[1,768,1536]{2,1,0:T(8,128)(2,1)}, u32[]{:S(2)}) copy-start(bf16[1,768,1536]{2,1,0:T(8,128)(2,1)} %param.10) | copy-start | bytes 7077892
  7.2 248.6 %all-reduce.4.cloned.1.call-start = ((), (), s32[]{:S(2)}) async-start(), calls=%async_computation | async-start | bytes 196608 | tf_op jit(solution)/shard_map/psum | solution.py:30
  11.2 458.9 %all-reduce.6.cloned.1.call-start = ((), (), s32[]{:S(2)}) async-start(), calls=%async_computation.1 | async-start | bytes 393216 | tf_op jit(solution)/shard_map/psum | solution.py:41
  256.9 213.1 %copy-start.2 = (f32[6,1536]{1,0:T(8,128)S(1)}, f32[6,1536]{1,0:T(8,128)}, u32[]{:S(2)}) copy-start(f32[6,1536]{1,0:T(8,128)} %param.13) | copy-start | bytes 110596
  257.0 213.1 %copy-start.3 = (f32[6,1536]{1,0:T(8,128)S(1)}, f32[6,1536]{1,0:T(8,128)}, u32[]{:S(2)}) copy-start(f32[6,1536]{1,0:T(8,128)} %param.14) | copy-start | bytes 110596
  257.0 215.1 %copy-start.7 = (u32[256]{0:T(256)S(1)}, u32[256]{0:T(256)}, u32[]{:S(2)}) copy-start(u32[256]{0:T(256)} %constant.38) | copy-start | bytes 3076
  257.0 216.3 %copy-start.4 = (bf16[1,5376]{1,0:T(2,128)(2,1)S(1)}, bf16[1,5376]{1,0:T(2,128)(2,1)}, u32[]{:S(2)}) copy-start(bf16[1,5376]{1,0:T(2,128)(2,1)} %param.15) | copy-start | bytes 32260
  257.0 902.7 %copy-start.5 = (f32[42]{0:T(128)S(1)}, f32[42]{0:T(128)}, u32[]{:S(2)}) copy-start(f32[42]{0:T(128)} %param.16) | copy-start | bytes 508
  257.0 902.7 %copy-start.6 = (f32[42]{0:T(128)S(1)}, f32[42]{0:T(128)}, u32[]{:S(2)}) copy-start(f32[42]{0:T(128)} %param.17) | copy-start | bytes 508
  260.1 1588.8 %all-gather.3.cloned.1.call-start = ((), (), s32[]{:S(2)}) async-start(), calls=%async_computation.2 | async-start | bytes 3170304 | tf_op jit(solution)/shard_map/all_gather | solution.py:52
Sparse Core Ops, SparseCore 0:
  14.1 241.6 all-reduce.3
  261.8 208.2 all-reduce.5
  475.0 112.6 all-gather.2
where the time goes:
time: 1860 us
  blocking collectives  1370 us (74%)
  waiting for transfers between devices  454 us (24%)
    psum x1, blocking collectives, on_device(): vec_total = lax.psum(vec_term, 'dp')  686 us
    unnamed x1, blocking collectives  682 us
    psum x1, waiting for transfers between devices, on_device(): row_total = lax.psum(row_part, ('dp', 'tensor'))  244 us
    psum x1, waiting for transfers between devices, on_device(): col_mean = lax.psum(col_part, 'dp') / replicas  210 us
  transfers between devices with their start and end apart: 3, of which 2 were waited for; matrix products, arithmetic and copies ran while one was open for 0% of the time, Pallas kernels for 0%

commit v1 on v0

--- a/solution.py
+++ b/solution.py
@@ -27,7 +27,7 @@
     row_part = jnp.dot(merged, query_b, preferred_element_type=jnp.float32)
     vec_term = vec_grads[0].astype(jnp.float32)
     shard_len = vec_master.shape[0]
-    row_total = lax.psum(row_part, ("dp", "tensor"))
+    row_total = jnp.sum(lax.all_gather(row_part, ("dp", "tensor")), axis=0)
     vec_total = lax.psum(vec_term, "dp")
     vec_mean = (
         lax.dynamic_slice_in_dim(vec_total, replica_index * shard_len, shard_len, 0) / replicas

time: 1860 us -> 1770 us (0.952)
  waiting for transfers between devices: 454 us -> 349 us
    psum x1 -> x0, waiting for transfers between devices: 244 us -> none  [on_device(): row_total = lax.psum(row_part, ('dp', 'tensor'))]
    all_gather x0 -> x1, waiting for transfers between devices: none -> 140 us  [on_device(): row_total = jnp.sum(lax.all_gather(row_part, ('dp', 'tensor')), axis=0)]
where the time goes in v1:
time: 1770 us
  blocking collectives  1370 us (77%)
  waiting for transfers between devices  349 us (20%)
  local copies, waits for them, and re-layouts  21.1 us (1%)
    psum x1, blocking collectives, on_device(): vec_total = lax.psum(vec_term, 'dp')  686 us
    unnamed x1, blocking collectives  682 us
    psum x1, waiting for transfers between devices, on_device(): col_mean = lax.psum(col_part, 'dp') / replicas  209 us
    all_gather x1, waiting for transfers between devices, on_device(): row_total = jnp.sum(lax.all_gather(row_part, ('dp', 'tensor')), axis=0)  140 us
  transfers between devices with their start and end apart: 3, of which 2 were waited for; matrix products, arithmetic and copies ran while one was open for 0% of the time, Pallas kernels for 0%

profile of v1, /device:TPU:0, one launch (start us, length us, event | category | flops | bytes accessed | tf_op | source)
XLA Modules:
  0.0 1770.9 jit_solution(14410806995569889100)
XLA Ops:
  7.2 0.0 copy-start
  7.2 0.0 all-gather.5.cloned.1.call-start
  7.2 3.8 fusion.9
  11.0 0.0 all-gather.5.cloned.1.call-update
  11.1 0.0 all-reduce.3.cloned.1.call-start
  11.1 140.1 %all-gather.5.cloned.1.call-done = f32[196608,32]{0,1:T(8,128)} async-done(((f32[768,32]{0,1:T(8,128)}), f32[196608,32]{0,1:T(8,128)}) %all-gather.5.cloned.1.call-update) | async-done | bytes 25165840 | tf_op jit(solution)/shard_map/all_gather | solution.py:30
  151.2 15.2 copy.16
  166.5 0.0 copy-start.1
  166.5 0.0 copy-start.2
  166.5 3.3 bitcast_reduce_fusion
  169.8 0.0 copy-done
  169.8 0.3 fusion.7
  170.1 0.0 copy-start.3
  170.2 0.0 copy-start.4
  170.2 0.0 copy-start.8
  170.2 0.0 copy-start.5
  170.2 0.0 copy-start.6
  170.2 0.0 copy-start.7
  170.2 1.4 fusion.11
  171.7 0.0 all-reduce.3.cloned.1.call-update
  171.7 0.0 all-gather.7.cloned.1.call-start
  171.7 208.8 %all-reduce.3.cloned.1.call-done = f32[1536,32]{0,1:T(8,128)} async-done(((f32[1536,32]{0,1:T(8,128)}), f32[1536,32]{0,1:T(8,128)}) %all-reduce.3.cloned.1.call-update) | async-done | bytes 196624 | tf_op jit(solution)/shard_map/psum | solution.py:41
  380.6 1.9 convert_bitcast_fusion
  382.5 0.0 all-gather.7.cloned.1.call-update
  382.5 0.6 dynamic-slice
  383.8 0.1 convert_reduce_fusion
  383.8 686.4 %psum.15 = f32[5376]{0:T(1024)S(1)} all-reduce(f32[5376]{0:T(1024)S(1)} %convert_reduce_fusion), channel_id=1, replica_groups=mesh['dp'=128,'tensor'=2] {'dp'}, use_global_device_ids=true, to_apply=%region_2.0 | all-reduce | flops 5376 | bytes 43008 | tf_op jit(solution)/shard_map/psum | solution.py:31
  1070.2 0.6 fusion.21
  1070.8 0.2 dynamic-update-slice
  1071.0 681.7 %all-reduce = bf16[5376]{0:T(1024)(128)(2,1)} all-reduce(bf16[5376]{0:T(1024)(128)(2,1)S(1)} %dynamic-update-slice), channel_id=1, replica_groups=mesh['dp'=128,'tensor'=2] {'dp'}, use_global_device_ids=true, to_apply=%add | all-reduce | flops 5376 | bytes 21504
  1752.8 6.6 fusion
  1759.4 5.0 reshape.26
  (10 shorter events, 0.0 us)
Async XLA Ops:
  7.2 162.7 %copy-start = (f32[32,32]{1,0:T(8,128)S(1)}, f32[32,32]{1,0:T(8,128)}, u32[]{:S(2)}) copy-start(f32[32,32]{1,0:T(8,128)} %param.12) | copy-start | bytes 12292
  7.2 144.1 %all-gather.5.cloned.1.call-start = ((), (), s32[]{:S(2)}) async-start(), calls=%async_computation.1 | async-start | bytes 25264128 | tf_op jit(solution)/shard_map/all_gather | solution.py:30
  11.1 369.5 %all-reduce.3.cloned.1.call-start = ((), (), s32[]{:S(2)}) async-start(), calls=%async_computation | async-start | bytes 393216 | tf_op jit(solution)/shard_map/psum | solution.py:41
  166.5 3.6 copy-start.1
  166.5 3.6 copy-start.2
  170.1 210.4 %copy-start.3 = (f32[6,1536]{1,0:T(8,128)S(1)}, f32[6,1536]{1,0:T(8,128)}, u32[]{:S(2)}) copy-start(f32[6,1536]{1,0:T(8,128)} %param.13) | copy-start | bytes 110596
  170.2 210.4 %copy-start.4 = (f32[6,1536]{1,0:T(8,128)S(1)}, f32[6,1536]{1,0:T(8,128)}, u32[]{:S(2)}) copy-start(f32[6,1536]{1,0:T(8,128)} %param.14) | copy-start | bytes 110596
  170.2 212.3 %copy-start.8 = (u32[256]{0:T(256)S(1)}, u32[256]{0:T(256)}, u32[]{:S(2)}) copy-start(u32[256]{0:T(256)} %constant.40) | copy-start | bytes 3076
  170.2 213.6 %copy-start.5 = (bf16[1,5376]{1,0:T(2,128)(2,1)S(1)}, bf16[1,5376]{1,0:T(2,128)(2,1)}, u32[]{:S(2)}) copy-start(bf16[1,5376]{1,0:T(2,128)(2,1)} %param.15) | copy-start | bytes 32260
  170.2 900.0 %copy-start.6 = (f32[42]{0:T(128)S(1)}, f32[42]{0:T(128)}, u32[]{:S(2)}) copy-start(f32[42]{0:T(128)} %param.16) | copy-start | bytes 508
  170.2 900.0 %copy-start.7 = (f32[42]{0:T(128)S(1)}, f32[42]{0:T(128)}, u32[]{:S(2)}) copy-start(f32[42]{0:T(128)} %param.17) | copy-start | bytes 508
  171.7 1587.7 %all-gather.7.cloned.1.call-start = ((), (), s32[]{:S(2)}) async-start(), calls=%async_computation.2 | async-start | bytes 3170304 | tf_op jit(solution)/shard_map/all_gather | solution.py:52
Sparse Core Ops, SparseCore 0:
  12.3 138.8 all-gather.4
  171.8 208.7 all-reduce.2
  385.4 112.6 all-gather.6

commit v2 on v0

--- a/solution.py
+++ b/solution.py
@@ -27,7 +27,7 @@
     row_part = jnp.dot(merged, query_b, preferred_element_type=jnp.float32)
     vec_term = vec_grads[0].astype(jnp.float32)
     shard_len = vec_master.shape[0]
-    row_total = lax.psum(row_part, ("dp", "tensor"))
+    row_total = lax.psum(lax.psum(row_part, "tensor"), "dp")
     vec_total = lax.psum(vec_term, "dp")
     vec_mean = (
         lax.dynamic_slice_in_dim(vec_total, replica_index * shard_len, shard_len, 0) / replicas

time: 1860 us -> 1870 us (level)
    psum x1 -> x2, waiting for transfers between devices: 244 us -> 247 us  [on_device(): row_total = lax.psum(lax.psum(row_part, 'tensor'), 'dp')]
  transfers between devices with their start and end apart: 3 -> 4, of which waited for: 2 -> 3; matrix products, arithmetic and copies ran while one was open for 0% -> 0% of each run, Pallas kernels for 0% -> 0%
where the time goes in v2:
time: 1870 us
  blocking collectives  1370 us (73%)
  waiting for transfers between devices  459 us (25%)
    psum x1, blocking collectives, on_device(): vec_total = lax.psum(vec_term, 'dp')  686 us
    unnamed x1, blocking collectives  682 us
    psum x2, waiting for transfers between devices, on_device(): row_total = lax.psum(lax.psum(row_part, 'tensor'), 'dp')  247 us
    psum x1, waiting for transfers between devices, on_device(): col_mean = lax.psum(col_part, 'dp') / replicas  212 us
  transfers between devices with their start and end apart: 4, of which 3 were waited for; matrix products, arithmetic and copies ran while one was open for 0% of the time, Pallas kernels for 0%

profile of v2, /device:TPU:0, one launch (start us, length us, event | category | flops | bytes accessed | tf_op | source)
XLA Modules:
  0.0 1865.1 jit_solution(8462455478323851707)
XLA Ops:
  7.2 0.0 copy-start
  7.2 0.0 all-reduce.5.cloned.1.call-start
  7.2 4.0 fusion.9
  11.2 0.0 all-reduce.5.cloned.1.call-update
  11.2 0.0 all-reduce.7.cloned.1.call-start
  11.3 30.2 %all-reduce.5.cloned.1.call-done = f32[768,32]{0,1:T(8,128)} async-done(((f32[768,32]{0,1:T(8,128)}), f32[768,32]{0,1:T(8,128)}) %all-reduce.5.cloned.1.call-update) | async-done | bytes 98320 | tf_op jit(solution)/shard_map/psum | solution.py:30
  41.5 0.0 all-reduce.7.cloned.1.call-update
  41.5 0.0 all-reduce.9.cloned.1.call-start
  41.6 216.7 %all-reduce.7.cloned.1.call-done = f32[768,32]{0,1:T(8,128)} async-done(((f32[768,32]{0,1:T(8,128)}), f32[768,32]{0,1:T(8,128)}) %all-reduce.7.cloned.1.call-update) | async-done | bytes 98320 | tf_op jit(solution)/shard_map/psum | solution.py:30
  258.3 0.0 copy-done
  258.3 1.2 fusion.7
  259.5 0.0 copy-done.1
  259.5 0.0 copy-start.2
  259.5 0.0 copy-start.3
  259.5 0.0 copy-start.7
  259.5 0.0 copy-start.4
  259.5 0.0 copy-start.5
  259.5 0.0 copy-start.6
  259.5 3.1 fusion.11
  262.7 0.0 all-reduce.9.cloned.1.call-update
  262.7 0.0 all-gather.3.cloned.1.call-start
  262.7 212.0 %all-reduce.9.cloned.1.call-done = f32[1536,32]{0,1:T(8,128)} async-done(((f32[1536,32]{0,1:T(8,128)}), f32[1536,32]{0,1:T(8,128)}) %all-reduce.9.cloned.1.call-update) | async-done | bytes 196624 | tf_op jit(solution)/shard_map/psum | solution.py:41
  474.7 1.9 convert_bitcast_fusion
  476.6 0.0 all-gather.3.cloned.1.call-update
  476.7 0.6 dynamic-slice
  477.9 0.1 convert_reduce_fusion
  478.0 686.3 %psum.31 = f32[5376]{0:T(1024)S(1)} all-reduce(f32[5376]{0:T(1024)S(1)} %convert_reduce_fusion), channel_id=1, replica_groups=mesh['dp'=128,'tensor'=2] {'dp'}, use_global_device_ids=true, to_apply=%region_3.0 | all-reduce | flops 5376 | bytes 43008 | tf_op jit(solution)/shard_map/psum | solution.py:31
  1164.3 0.6 fusion.21
  1164.9 0.2 dynamic-update-slice
  1165.1 681.7 %all-reduce = bf16[5376]{0:T(1024)(128)(2,1)} all-reduce(bf16[5376]{0:T(1024)(128)(2,1)S(1)} %dynamic-update-slice), channel_id=1, replica_groups=mesh['dp'=128,'tensor'=2] {'dp'}, use_global_device_ids=true, to_apply=%add | all-reduce | flops 5376 | bytes 21504
  1846.9 6.6 fusion
  1853.5 5.0 reshape.25
  (9 shorter events, 0.0 us)
Async XLA Ops:
  7.2 251.1 %copy-start = (f32[32,32]{1,0:T(8,128)S(1)}, f32[32,32]{1,0:T(8,128)}, u32[]{:S(2)}) copy-start(f32[32,32]{1,0:T(8,128)} %param.12) | copy-start | bytes 12292
  7.2 252.3 %copy-start.1 = (bf16[1,768,1536]{2,1,0:T(8,128)(2,1)S(1)}, bf16[1,768,1536]{2,1,0:T(8,128)(2,1)}, u32[]{:S(2)}) copy-start(bf16[1,768,1536]{2,1,0:T(8,128)(2,1)} %param.10) | copy-start | bytes 7077892
  7.2 34.3 %all-reduce.5.cloned.1.call-start = ((), (), s32[]{:S(2)}) async-start(), calls=%async_computation | async-start | bytes 196608 | tf_op jit(solution)/shard_map/psum | solution.py:30
  11.2 247.1 %all-reduce.7.cloned.1.call-start = ((), (), s32[]{:S(2)}) async-start(), calls=%async_computation.1 | async-start | bytes 196608 | tf_op jit(solution)/shard_map/psum | solution.py:30
  41.5 433.2 %all-reduce.9.cloned.1.call-start = ((), (), s32[]{:S(2)}) async-start(), calls=%async_computation.2 | async-start | bytes 393216 | tf_op jit(solution)/shard_map/psum | solution.py:41
  259.5 215.3 %copy-start.2 = (f32[6,1536]{1,0:T(8,128)S(1)}, f32[6,1536]{1,0:T(8,128)}, u32[]{:S(2)}) copy-start(f32[6,1536]{1,0:T(8,128)} %param.13) | copy-start | bytes 110596
  259.5 215.2 %copy-start.3 = (f32[6,1536]{1,0:T(8,128)S(1)}, f32[6,1536]{1,0:T(8,128)}, u32[]{:S(2)}) copy-start(f32[6,1536]{1,0:T(8,128)} %param.14) | copy-start | bytes 110596
  259.5 217.2 %copy-start.7 = (u32[256]{0:T(256)S(1)}, u32[256]{0:T(256)}, u32[]{:S(2)}) copy-start(u32[256]{0:T(256)} %constant.38) | copy-start | bytes 3076
  259.5 218.4 %copy-start.4 = (bf16[1,5376]{1,0:T(2,128)(2,1)S(1)}, bf16[1,5376]{1,0:T(2,128)(2,1)}, u32[]{:S(2)}) copy-start(bf16[1,5376]{1,0:T(2,128)(2,1)} %param.15) | copy-start | bytes 32260
  259.5 904.8 %copy-start.5 = (f32[42]{0:T(128)S(1)}, f32[42]{0:T(128)}, u32[]{:S(2)}) copy-start(f32[42]{0:T(128)} %param.16) | copy-start | bytes 508
  259.5 904.8 %copy-start.6 = (f32[42]{0:T(128)S(1)}, f32[42]{0:T(128)}, u32[]{:S(2)}) copy-start(f32[42]{0:T(128)} %param.17) | copy-start | bytes 508
  262.7 1590.8 %all-gather.3.cloned.1.call-start = ((), (), s32[]{:S(2)}) async-start(), calls=%async_computation.3 | async-start | bytes 3170304 | tf_op jit(solution)/shard_map/all_gather | solution.py:52
Sparse Core Ops, SparseCore 0:
  11.3 30.0 all-reduce.4
  46.9 211.2 all-reduce.6
  265.2 209.4 all-reduce.8
  478.8 112.9 all-gather.2
